TPU v7x, 32 devices: a whole 2x2x4 slice. The times are simulated.
32 devices in a mesh: band: 8 (over z, y), mode: 4 (over x, core).
Axes of the slice: x: 2, y: 2, z: 4, core: 2. Of those that a mesh axis runs over, the one named last changes fastest.
Arguments:
- velocity: bfloat16 [1, 8192, 1024], P(None, ('band', 'mode')), may hold values from -6 to 6
- radiation_modes: bfloat16 [8192, 1024], P('band', 'mode'), may hold values from -0.125 to 0.125
- resistance: float32 [8, 1024, 1024], P('band', None, 'mode'), as said below
- mode_ranks: int32 [8], P('band'), may hold values from 128 to 1024, as said below
- freq_table: int32 [512], replicated, may hold values from 0 to 511, each once
Outputs:
- adjoint_force: bfloat16 [1, 8192, 1024], P(None, ('band', 'mode'))
Inputs may be any that keep to these rules, and one draw needn't show every extreme that they name: `resistance`: each band's matrix is symmetric. `mode_ranks`: the ranks never fall with the band index; the first band keeps 1024 // 8 modes and the last 1024.
All inputs are finite; a program needn't handle non-finite values.
Results may differ from a plain program's by a relative error of at most 0.015.
Values may be sent and summed in bfloat16 or wider, within the bound.
A program may use at most 64 MiB of HBM per device.

v0:
```python
import math

import jax
import jax.numpy as jnp
from jax import lax
from jax.sharding import PartitionSpec as P


def make_table(freq_table, step_count):
    times = jnp.arange(step_count, dtype=jnp.int32)
    phases = times[:, None] * freq_table[None, :] % step_count
    angles = phases.astype(jnp.float32) * (2.0 * math.pi / step_count)
    norming = 1.0 / math.sqrt(step_count)
    table = jnp.stack([jnp.cos(angles), -jnp.sin(angles)], axis=1) * norming
    return table.astype(jnp.bfloat16)


def add_sources(received):
    return jnp.sum(received, axis=0)


def per_device(velocity, radiation_modes, resistance, mode_ranks, freq_table):
    step_count = velocity.shape[2]
    mode_cols = radiation_modes.shape[1]
    dft_table = make_table(freq_table, step_count)
    spectra = jnp.einsum(
        "wpt,tcf->wpcf", velocity, dft_table, preferred_element_type=jnp.float32
    ).astype(jnp.bfloat16)
    partial_value = jnp.einsum(
        "wpcf,pr->wrcf",
        lax.all_gather(spectra, "mode", axis=1, tiled=True),
        radiation_modes,
        preferred_element_type=jnp.float32,
    )
    coefficients = add_sources(
        lax.all_to_all(
            partial_value[None].astype(jnp.bfloat16),
            "band",
            split_axis=4,
            concat_axis=0,
            tiled=True,
        ).astype(jnp.float32)
    )
    offset = lax.axis_index("mode") * mode_cols
    rank_here = mode_ranks[0]
    kept_mask = (offset + jnp.arange(mode_cols, dtype=jnp.int32) < rank_here).astype(jnp.float32)
    kept_mask = kept_mask[None, :, None, None]
    coefficients = coefficients * kept_mask
    matrix = resistance[0]
    partial_terms = jnp.einsum(
        "ij,wjcf->wicf", matrix, coefficients, precision=lax.Precision.HIGHEST
    )
    forcing = lax.psum_scatter(
        partial_terms.astype(jnp.bfloat16), "mode", scatter_dimension=1, tiled=True
    ).astype(jnp.float32)
    forcing = (2.0 * forcing * kept_mask).astype(jnp.bfloat16)
    collected = lax.all_gather(forcing, "mode", axis=1, tiled=True)
    collected = lax.all_gather(collected, "band", axis=3, tiled=True)
    own_basis = lax.all_to_all(radiation_modes, "mode", split_axis=0, concat_axis=1, tiled=True)
    surface_force = jnp.einsum(
        "pr,wrcf->wpcf", own_basis, collected, preferred_element_type=jnp.float32
    ).astype(jnp.bfloat16)
    history = jnp.einsum(
        "wpcf,tcf->wpt", surface_force, dft_table, preferred_element_type=jnp.float32
    )
    return history.astype(jnp.bfloat16)


def solution(mesh):
    placed = (
        P(None, ("band", "mode"), None),
        P("band", "mode"),
        P("band", None, "mode"),
        P("band"),
        P(),
    )
    return jax.shard_map(
        per_device,
        mesh=mesh,
        in_specs=placed,
        out_specs=P(None, ("band", "mode"), None),
        check_vma=False,
    )
```

profile of v0, /device:TPU:0, one launch (start us, length us, event | category | flops | bytes accessed | tf_op | source)
XLA Modules:
  0.0 158.5 jit_solution(3879735066893673971)
XLA Ops:
  6.5 0.0 copy-start
  6.5 0.0 copy-start.4
  6.5 0.0 all-gather.6.cloned.1.call-start
  6.5 9.1 %fusion.21 = (f32[1024,1,512]{0,2,1:T(8,128)S(1)}, f32[1024,1,512]{0,2,1:T(8,128)S(1)}) fusion(s32[512]{0:T(512)} %param.9), kind=kLoop, calls=%fused_computation.27 | loop fusion | flops 7864320 | bytes 4196352 | tf_op jit(solution)/shard_map/cos | solution.py:14
  15.7 0.0 copy-start.1
  15.7 0.0 copy-start.2
  15.7 1.3 copy-done.1
  17.0 0.6 copy-done.2
  17.6 0.0 copy-done.4
  17.7 1.6 fusion.13
  19.2 0.0 all-gather.6.cloned.1.call-update
  19.2 25.7 %all-gather.6.cloned.1.call-done = bf16[1024,2,512]{0,2,1:T(8,128)(2,1)} async-done(((bf16[256,2,512]{0,2,1:T(8,128)(2,1)}), bf16[1024,2,512]{0,2,1:T(8,128)(2,1)}) %all-gather.6.cloned.1.call-update) | async-done | bytes 2097168 | tf_op jit(solution)/shard_map/all_gather | solution.py:31
  44.9 0.0 copy-done.3
  44.9 2.3 %fusion.14 = bf16[1,1,256,2,512]{2,4,3,1,0:T(8,128)(2,1)S(1)} fusion(bf16[1024,2,512]{0,2,1:T(8,128)(2,1)} %all-gather.6.cloned.1.call-done, bf16[1024,256]{1,0:T(8,128)(2,1)S(1)} %copy-done.3), kind=kOutput, calls=%fused_computation.20 | convolution fusion | flops 537133056 | bytes 3145728 | tf_op jit(solution)/shard_map/wpcf,pr->wrcf/dot_general | solution.py:29
  47.2 1.3 copy.16
  48.6 5.5 %all-to-all-start = ((bf16[1,1,256,2,512]{2,3,1,0,4:T(2,128)(2,1)}), bf16[1,1,256,2,512]{2,3,1,0,4:T(2,128)(2,1)S(1)}, u32[]{:S(2)}, u32[]{:S(2)}) async-start(bf16[1,1,256,2,512]{2,3,1,0,4:T(2,128)(2,1)} %copy.16), calls=%async_computation | async-start | bytes 1048576 | tf_op jit(solution)/shard_map/all_to_all | solution.py:36
  54.1 0.2 reduce-scatter.2.cloned.1.call-start
  55.0 14.0 %all-to-all-done = bf16[1,1,256,2,512]{2,3,1,0,4:T(2,128)(2,1)S(1)} async-done(((bf16[1,1,256,2,512]{2,3,1,0,4:T(2,128)(2,1)}), bf16[1,1,256,2,512]{2,3,1,0,4:T(2,128)(2,1)S(1)}, u32[]{:S(2)}, u32[]{:S(2)}) %all-to-all-start) | async-done | bytes 524320 | tf_op jit(solution)/shard_map/all_to_all | solution.py:36
  69.0 0.5 convert_reduce_fusion
  69.4 0.0 copy-done
  69.5 1.9 %fusion.19 = bf16[1,1024,2,64]{1,3,2,0:T(8,128)(2,1)} fusion(f32[1,1024,256]{2,1,0:T(8,128)S(1)} %copy-done, f32[256,2,64]{0,1,2:T(2,128)S(1)} %convert_reduce_fusion, f32[256]{0:T(256)S(1)} %fusion.30), kind=kOutput, calls=%fused_computation.24 | convolution fusion | flops 402817024 | bytes 1442816 | tf_op jit(solution)/shard_map/ij,wjcf->wicf/dot_general | solution.py:50
  71.4 0.0 reduce-scatter.2.cloned.1.call-update
  71.4 0.0 all-gather.4.cloned.1.call-start
  71.5 18.3 %reduce-scatter.2.cloned.1.call-done = bf16[1,256,2,64]{1,3,2,0:T(8,128)(2,1)} async-done(((bf16[1,1024,2,64]{1,3,2,0:T(8,128)(2,1)}), bf16[1,256,2,64]{1,3,2,0:T(8,128)(2,1)}) %reduce-scatter.2.cloned.1.call-update) | async-done | bytes 65552 | tf_op jit(solution)/shard_map/reduce_scatter | solution.py:53
  89.7 0.9 multiply_convert_fusion
  90.6 6.2 %all_gather.10 = bf16[1,1024,2,64]{1,3,2,0:T(8,128)(2,1)} all-gather(bf16[1,256,2,64]{1,3,2,0:T(8,128)(2,1)S(1)} %multiply_convert_fusion), channel_id=1, replica_groups=mesh['band'=8,'mode'=4] {'mode'}, dimensions={1}, use_global_device_ids=true | all-gather | bytes 327680 | tf_op jit(solution)/shard_map/all_gather | solution.py:57
  96.8 0.0 all-gather.4.cloned.1.call-update
  96.8 11.2 %all_to_all.28 = bf16[4,256,256]{2,1,0:T(8,128)(2,1)S(1)} all-to-all(bf16[4,256,256]{2,1,0:T(8,128)(2,1)S(1)} %bitcast.57), channel_id=1, replica_groups=mesh['band'=8,'mode'=4] {'mode'}, dimensions={0} | all-to-all | bytes 1048576 | tf_op jit(solution)/shard_map/all_to_all | solution.py:59
  108.1 0.4 copy.18
  108.5 0.4 reshape.162
  108.8 37.2 %all-gather.4.cloned.1.call-done = bf16[1,1024,2,512]{1,3,2,0:T(8,128)(2,1)} async-done(((bf16[1,1024,2,64]{1,3,2,0:T(8,128)(2,1)}), bf16[1,1024,2,512]{1,3,2,0:T(8,128)(2,1)}) %all-gather.4.cloned.1.call-update) | async-done | bytes 2097168 | tf_op jit(solution)/shard_map/all_gather | solution.py:58
  146.1 5.9 %fusion.18 = bf16[1,256,1024]{2,1,0:T(8,128)(2,1)} fusion(bf16[256,1024,1]{1,0,2:T(8,128)(2,1)S(1)} %reshape.162, bf16[1,1024,2,512]{1,3,2,0:T(8,128)(2,1)} %all-gather.4.cloned.1.call-done, f32[1024,1,512]{0,2,1:T(8,128)} %copy-done.2, f32[1024,1,512]{0,2,1:T(8,128)} %copy-done.1), kind=kOutput, calls=%fused_computation.22 | convolution fusion | flops 1077411840 | bytes 7340032 | tf_op jit(solution)/shard_map/wpcf,tcf->wpt/dot_general | solution.py:63
  (3 shorter events, 0.0 us)
Async XLA Ops:
  6.5 62.9 %copy-start = (f32[1,1024,256]{2,1,0:T(8,128)S(1)}, f32[1,1024,256]{2,1,0:T(8,128)}, u32[]{:S(2)}) copy-start(f32[1,1024,256]{2,1,0:T(8,128)} %param.7) | copy-start | bytes 3145732
  6.5 11.1 %copy-start.4 = (bf16[1,256,1024]{2,1,0:T(8,128)(2,1)S(1)}, bf16[1,256,1024]{2,1,0:T(8,128)(2,1)}, u32[]{:S(2)}) copy-start(bf16[1,256,1024]{2,1,0:T(8,128)(2,1)} %param.5) | copy-start | bytes 1572868
  6.5 38.4 %all-gather.6.cloned.1.call-start = ((), (), s32[]{:S(2)}) async-start(), calls=%async_computation.5 | async-start | bytes 2621440 | tf_op jit(solution)/shard_map/all_gather | solution.py:31
  15.7 1.3 copy-start.1
  15.7 1.9 %copy-start.2 = (f32[1024,1,512]{0,2,1:T(8,128)}, f32[1024,1,512]{0,2,1:T(8,128)S(1)}, u32[]{:S(2)}) copy-start(f32[1024,1,512]{0,2,1:T(8,128)S(1)} %get-tuple-element.6) | copy-start | bytes 6291460
  17.7 27.3 %copy-start.3 = (bf16[1024,256]{1,0:T(8,128)(2,1)S(1)}, bf16[1024,256]{1,0:T(8,128)(2,1)}, u32[]{:S(2)}) copy-start(bf16[1024,256]{1,0:T(8,128)(2,1)} %param.6) | copy-start | bytes 1572868
  48.6 20.4 %all-to-all-start = ((bf16[1,1,256,2,512]{2,3,1,0,4:T(2,128)(2,1)}), bf16[1,1,256,2,512]{2,3,1,0,4:T(2,128)(2,1)S(1)}, u32[]{:S(2)}, u32[]{:S(2)}) async-start(bf16[1,1,256,2,512]{2,3,1,0,4:T(2,128)(2,1)} %copy.16), calls=%async_computation | async-start | bytes 1048576 | tf_op jit(solution)/shard_map/all_to_all | solution.py:36
  54.1 35.7 %reduce-scatter.2.cloned.1.call-start = ((), (), s32[]{:S(2)}) async-start(), calls=%async_computation.3 | async-start | bytes 327680 | tf_op jit(solution)/shard_map/reduce_scatter | solution.py:53
  71.4 74.7 %all-gather.4.cloned.1.call-start = ((), (), s32[]{:S(2)}) async-start(), calls=%async_computation.4 | async-start | bytes 2359296 | tf_op jit(solution)/shard_map/all_gather | solution.py:58
Sparse Core Ops, SparseCore 0:
  19.4 25.5 all-gather.5
  71.5 18.1 reduce-scatter.1
  97.0 49.0 all-gather.3
where the time goes:
time: 159 us
  waiting for transfers between devices  95.3 us (60%)
  blocking collectives  17.4 us (11%)
  between operations  13.8 us (9%)
  matrix products  11.7 us (7%)
  other arithmetic  10.5 us (7%)
  starting transfers between devices  5.78 us (4%)
  local copies, waits for them, and re-layouts  4.06 us (3%)
    all_gather x1, waiting for transfers between devices, per_device(): collected = lax.all_gather(collected, 'band', axis=3, tiled=True)  37.2 us
    all_gather x1, waiting for transfers between devices, per_device(): lax.all_gather(spectra, 'mode', axis=1, tiled=True)  25.7 us
    reduce_scatter x1, waiting for transfers between devices, per_device(): lax.psum_scatter(partial_terms.astype(jnp.bfloat16), 'mode', scatter_dime...  18.3 us
    all_to_all x1, waiting for transfers between devices, per_device(): lax.all_to_all(partial_value[None].astype(jnp.bfloat16), 'band', split_ax...  14 us
    all_to_all x1, blocking collectives, per_device(): lax.all_to_all(radiation_modes, 'mode', split_axis=0, concat_axis=1, tile...  11.2 us
    cos x1, other arithmetic, make_table(): table = jnp.stack([jnp.cos(angles), -jnp.sin(angles)], axis=1) * norming  9.14 us
    all_gather x1, blocking collectives, per_device(): collected = lax.all_gather(forcing, 'mode', axis=1, tiled=True)  6.23 us
    dot_general x1, matrix products, per_device(): jnp.einsum('wpcf,tcf->wpt', surface_force, dft_table, preferred_element_t...  5.95 us
  transfers between devices with their start and end apart: 4, of which 4 were waited for; matrix products, arithmetic and copies ran while one was open for 0% of the time, Pallas kernels for 0%

commit v1 on v0

--- a/solution.py
+++ b/solution.py
@@ -1,9 +1,306 @@
+import functools
 import math
 
 import jax
 import jax.numpy as jnp
 from jax import lax
+from jax.experimental import pallas as pl
+from jax.experimental.pallas import tpu as pltpu
 from jax.sharding import PartitionSpec as P
+
+MESH = pl.DeviceIdType.MESH
+HALF_ROWS = 32
+
+
+def cosine_of(phase, period):
+    wrapped = phase & (period - 1)
+    folded = jnp.minimum(wrapped, period - wrapped)
+    flip = folded > period // 4
+    folded = jnp.where(flip, period // 2 - folded, folded)
+    x = folded.astype(jnp.float32) * (2.0 * math.pi / period)
+    y = x * x
+    value = jnp.full_like(y, 1.0 / math.factorial(16))
+    for n in range(14, -1, -2):
+        sign = -1.0 if n % 4 else 1.0
+        value = value * y + sign / math.factorial(n)
+    return jnp.where(flip, -value, value)
+
+
+def ordered_offsets(n):
+    offsets = [0]
+    for step in range(1, n // 2 + 1):
+        offsets.append(step)
+        if n - step != step:
+            offsets.append(n - step)
+    return offsets[:n]
+
+
+def fused_kernel(
+    nb, nm, vel_ref, modes_ref, res_ref, rank_ref, freq_ref, out_ref,
+    table, trig, modes_t, res_hi, res_lo, spec, part, rs, coef, force, basis, acc,
+    bar_unused, sx_s, sx_r, sm_s, sm_r, sf_s, sf_r, rs_s, rs_r, k_s, k_r, ob_s, ob_r,
+    f_s, f_r, fx_s, fx_r, fm_s, fm_r, ff_s, ff_r,
+):
+    b = lax.axis_index("band")
+    m = lax.axis_index("mode")
+    mate = m + 1 - 2 * (m % 2)
+    cross = (m + 2) % nm
+    diag = (mate + 2) % nm
+    patches, steps = vel_ref.shape
+    cols = table.shape[2]
+    mode_cols = modes_ref.shape[1]
+
+    def band_at(offset):
+        return (b + offset) % nb
+
+    def to_mode(src, dst, send, recv, target):
+        return pltpu.make_async_remote_copy(
+            src_ref=src, dst_ref=dst, send_sem=send, recv_sem=recv,
+            device_id={"mode": target}, device_id_type=MESH)
+
+    def to_band(src, dst, send, recv, target):
+        return pltpu.make_async_remote_copy(
+            src_ref=src, dst_ref=dst, send_sem=send, recv_sem=recv,
+            device_id={"band": target}, device_id_type=MESH)
+
+    barrier = pltpu.get_barrier_semaphore()
+    for off in range(1, nm):
+        pl.semaphore_signal(barrier, inc=1, device_id={"mode": (m + off) % nm}, device_id_type=MESH)
+    for off in range(1, nb):
+        pl.semaphore_signal(barrier, inc=1, device_id={"band": band_at(off)}, device_id_type=MESH)
+
+    blocks = steps // HALF_ROWS
+    norming = 1.0 / math.sqrt(steps)
+
+    def build(k):
+        freq = freq_ref[k]
+        shift = freq_ref[nb]
+        rows = lax.broadcasted_iota(jnp.int32, (HALF_ROWS, cols), 0)
+        big = lax.broadcasted_iota(jnp.int32, (blocks, cols), 0) * HALF_ROWS
+        low = rows * freq + shift
+        high = big * freq
+        quarter = steps // 4
+        cos_low = cosine_of(low, steps) * norming
+        sin_low = cosine_of(low - quarter, steps) * norming
+        trig[0] = cosine_of(high, steps)
+        trig[1] = cosine_of(high - quarter, steps)
+        for a in range(blocks):
+            row = trig[0, pl.ds(a, 1), :] * cos_low - trig[1, pl.ds(a, 1), :] * sin_low
+            table[k, pl.ds(a * HALF_ROWS, HALF_ROWS), :] = row.astype(jnp.bfloat16)
+
+    def spectra(k):
+        build(k)
+        spec[k, m] = jnp.dot(
+            vel_ref[...], table[k], preferred_element_type=jnp.float32
+        ).astype(jnp.bfloat16)
+
+    order = [(i + 1) % nb for i in range(nb)]
+    spectra(band_at(order[0]))
+    pl.semaphore_wait(barrier, nm - 1 + nb - 1)
+
+    def s_cross(k):
+        return to_mode(spec.at[k, m], spec.at[k, m], sx_s.at[k], sx_r.at[k], cross)
+
+    def s_mate(k):
+        return to_mode(spec.at[k, m], spec.at[k, m], sm_s.at[k], sm_r.at[k], mate)
+
+    def s_fwd(k):
+        return to_mode(spec.at[k, cross], spec.at[k, cross], sf_s.at[k], sf_r.at[k], mate)
+
+    def spec_step(i, _):
+        k = (b + 1 + i) % nb
+        s_cross(k).start()
+        s_mate(k).start()
+
+        nxt = (b + 2 + i) % nb
+        spectra(nxt)
+        return 0
+
+    lax.fori_loop(0, nb - 1, spec_step, 0)
+    s_cross(b).start()
+    s_mate(b).start()
+
+    def basis_copy(off):
+        target = (m + off) % nm
+        rows = pl.ds(pl.multiple_of(target * patches, patches), patches)
+        return to_mode(modes_ref.at[rows], basis.at[m], ob_s.at[off], ob_r.at[off], target)
+
+    for off in range(1, nm):
+        basis_copy(off).start()
+    modes_t[...] = modes_ref[...].T
+
+    def partial(k):
+        return jnp.dot(
+            modes_t[...], spec[k].reshape(nm * patches, cols), preferred_element_type=jnp.float32)
+
+    def rs_copy(k):
+        return to_band(part.at[k], rs.at[b], rs_s.at[k], rs_r.at[b], k)
+
+    def rs_arrival(k):
+        return to_band(part.at[k], rs.at[k], rs_s.at[k], rs_r.at[k], k)
+
+    def arrive(k):
+        s_cross(k).wait_recv()
+        s_fwd(k).start()
+
+    def finish(k):
+        s_mate(k).wait_recv()
+        s_fwd(k).wait_recv()
+
+    def part_step(i, _):
+        k = (b + 1 + i) % nb
+        arrive((b + 2 + i) % nb)
+        finish(k)
+        part[k] = partial(k).astype(jnp.bfloat16)
+        rs_copy(k).start()
+        return 0
+
+    arrive(band_at(1))
+    lax.fori_loop(0, nb - 1, part_step, 0)
+    wide = res_ref[...].T
+    narrow = wide.astype(jnp.bfloat16)
+    res_hi[...] = narrow
+    res_lo[...] = (wide - narrow.astype(jnp.float32)).astype(jnp.bfloat16)
+    finish(b)
+    total = partial(b)
+    for off in range(1, nb):
+        k = band_at(nb - off)
+        rs_arrival(k).wait_recv()
+        total = total + rs[k].astype(jnp.float32)
+    kept = lax.broadcasted_iota(jnp.int32, (mode_cols, cols), 0) + m * mode_cols < rank_ref[0]
+    total = jnp.where(kept, total, 0.0)
+    coef[m] = total.astype(jnp.bfloat16)
+
+    def k_copy(off):
+        return to_mode(coef.at[m], coef.at[m], k_s.at[off], k_r.at[off], (m + off) % nm)
+
+    def k_arrival(off):
+        source = (m + nm - off) % nm
+        return to_mode(coef.at[source], coef.at[source], k_s.at[off], k_r.at[off], source)
+
+    for off in range(1, nm):
+        k_copy(off).start()
+    for off in range(1, nm):
+        k_arrival(off).wait_recv()
+    coefs = coef[...].reshape(nm * mode_cols, cols)
+    forcing = jnp.dot(res_hi[...], coefs, preferred_element_type=jnp.float32) + jnp.dot(
+        res_lo[...], coefs, preferred_element_type=jnp.float32)
+    forcing = jnp.where(kept, 2.0 * forcing, 0.0)
+    force[b, m] = forcing.astype(jnp.bfloat16)
+
+    def f_copy(k):
+        return to_band(force.at[b, m], force.at[b, m], f_s.at[k], f_r.at[b], k)
+
+    def f_arrival(k):
+        return to_band(force.at[k, m], force.at[k, m], f_s.at[k], f_r.at[k], k)
+
+    def f_cross(k):
+        return to_mode(force.at[k, m], force.at[k, m], fx_s.at[k], fx_r.at[k], cross)
+
+    def f_mate(k):
+        return to_mode(force.at[k, m], force.at[k, m], fm_s.at[k], fm_r.at[k], mate)
+
+    def f_fwd(k):
+        return to_mode(force.at[k, cross], force.at[k, cross], ff_s.at[k], ff_r.at[k], mate)
+
+    offsets = ordered_offsets(nb)
+    for off in offsets[1:]:
+        f_copy(band_at(off)).start()
+    f_cross(b).start()
+    f_mate(b).start()
+
+    for off in range(1, nm):
+        source = (m + nm - off) % nm
+        to_mode(basis.at[source], basis.at[source], ob_s.at[off], ob_r.at[off], source).wait_recv()
+    basis[m] = modes_ref[pl.ds(pl.multiple_of(m * patches, patches), patches), :]
+
+    def surface(k):
+        value = jnp.dot(basis[0], force[k, 0], preferred_element_type=jnp.float32)
+        for j in range(1, nm):
+            value = value + jnp.dot(basis[j], force[k, j], preferred_element_type=jnp.float32)
+        return value.astype(jnp.bfloat16)
+
+    def history(k):
+        f_mate(k).wait_recv()
+        f_fwd(k).wait_recv()
+        return lax.dot_general(
+            surface(k), table[k], (((1,), (1,)), ((), ())), preferred_element_type=jnp.float32)
+
+    for i in range(nb + 2):
+        if 1 <= i < nb:
+            k = band_at(offsets[i])
+            f_arrival(k).wait_recv()
+            f_cross(k).start()
+            f_mate(k).start()
+        if 1 <= i <= nb:
+            k = band_at(offsets[i - 1])
+            f_cross(k).wait_recv()
+            f_fwd(k).start()
+        if i >= 2:
+            k = band_at(offsets[i - 2])
+            term = history(k)
+            if i == 2:
+                acc[...] = term
+            elif i < nb + 1:
+                acc[...] += term
+            else:
+                out_ref[...] = (acc[...] + term).astype(out_ref.dtype)
+
+    def drain(k, _):
+        for copy in (s_cross, s_mate, s_fwd, f_cross, f_mate, f_fwd):
+            copy(k).wait_send()
+        return 0
+
+    lax.fori_loop(0, nb, drain, 0)
+    for off in range(1, nb):
+        k = band_at(off)
+        rs_copy(k).wait_send()
+        f_copy(k).wait_send()
+    for off in range(1, nm):
+        basis_copy(off).wait_send()
+        k_copy(off).wait_send()
+
+
+def fused(mesh, velocity, radiation_modes, resistance, mode_ranks, freq_table):
+    nb, nm = mesh.shape["band"], mesh.shape["mode"]
+    patches, steps = velocity.shape[1:]
+    mode_cols = radiation_modes.shape[1]
+    modes = nm * mode_cols
+    slots = freq_table.shape[0] // nb
+    cols = 2 * slots
+    by_band = freq_table.reshape(nb, 1, slots)
+    freq_cols = jnp.concatenate([by_band, by_band], axis=2)
+    shift = jnp.where(jnp.arange(cols, dtype=jnp.int32) < slots, 0, steps // 4)
+    freq_cols = jnp.concatenate([freq_cols, shift.reshape(1, 1, cols).astype(jnp.int32)], axis=0)
+    bf16, f32 = jnp.bfloat16, jnp.float32
+    dma = lambda n: pltpu.SemaphoreType.DMA((n,))
+    vmem = pl.BlockSpec(memory_space=pltpu.VMEM)
+    out = pl.pallas_call(
+        functools.partial(fused_kernel, nb, nm),
+        out_shape=jax.ShapeDtypeStruct((patches, steps), bf16),
+        in_specs=[vmem, vmem, vmem, pl.BlockSpec(memory_space=pltpu.SMEM), vmem],
+        out_specs=vmem,
+        scratch_shapes=[
+            pltpu.VMEM((nb, steps, cols), bf16),
+            pltpu.VMEM((2, steps // HALF_ROWS, cols), f32),
+            pltpu.VMEM((mode_cols, nm * patches), bf16),
+            pltpu.VMEM((mode_cols, modes), bf16),
+            pltpu.VMEM((mode_cols, modes), bf16),
+            pltpu.VMEM((nb, nm, patches, cols), bf16),
+            pltpu.VMEM((nb, mode_cols, cols), bf16),
+            pltpu.VMEM((nb, mode_cols, cols), bf16),
+            pltpu.VMEM((nm, mode_cols, cols), bf16),
+            pltpu.VMEM((nb, nm, mode_cols, cols), bf16),
+            pltpu.VMEM((nm, patches, mode_cols), bf16),
+            pltpu.VMEM((patches, steps), f32),
+            pltpu.SemaphoreType.REGULAR,
+        ]
+        + [dma(nb) for _ in range(8)]
+        + [dma(nm) for _ in range(4)]
+        + [dma(nb) for _ in range(8)],
+        compiler_params=pltpu.CompilerParams(collective_id=0, has_side_effects=True),
+    )(velocity[0], radiation_modes, resistance[0], mode_ranks, freq_cols)
+    return out[None]
 
 
 def make_table(freq_table, step_count):
@@ -74,8 +371,21 @@
         P("band"),
         P(),
     )
+    nb, nm = mesh.shape["band"], mesh.shape["mode"]
+
+    def body(velocity, radiation_modes, resistance, mode_ranks, freq_table):
+        windows, patches, steps = velocity.shape
+        mode_cols = radiation_modes.shape[1]
+        cols = 2 * (freq_table.shape[0] // nb)
+        tiled = (
+            windows == 1 and nm == 4 and nb > 1 and cols % 128 == 0 and mode_cols % 128 == 0
+            and patches % 128 == 0 and steps % 128 == 0 and steps & (steps - 1) == 0
+        )
+        args = (velocity, radiation_modes, resistance, mode_ranks, freq_table)
+        return fused(mesh, *args) if tiled else per_device(*args)
+
     return jax.shard_map(
-        per_device,
+        body,
         mesh=mesh,
         in_specs=placed,
         out_specs=P(None, ("band", "mode"), None),

time: 159 us -> 60.3 us (0.38)
  waiting for transfers between devices: 95.3 us -> 0 us
  Pallas kernels: 0 us -> 55.7 us
  blocking collectives: 17.4 us -> 0 us
  between operations: 13.8 us -> 0.68 us
  matrix products: 11.7 us -> 0 us
  other arithmetic: 10.5 us -> 0.68 us
  starting transfers between devices: 5.78 us -> 0 us
    all_gather x2 -> x0, waiting for transfers between devices: 62.9 us -> none  [the longest x1 37.2 us: per_device(): collected = lax.all_gather(collected, 'band', axis=3, tiled=True)]
    pallas_call x0 -> x1, Pallas kernels: none -> 55.7 us  [fused(): pl.pallas_call(functools.partial(fused_kernel, nb, nm), out_shape=jax.Sha...]
    reduce_scatter x1 -> x0, waiting for transfers between devices: 18.3 us -> none  [per_device(): lax.psum_scatter(partial_terms.astype(jnp.bfloat16), 'mode', scatter_dime...]
    all_to_all x1 -> x0, waiting for transfers between devices: 14 us -> none  [per_device(): lax.all_to_all(partial_value[None].astype(jnp.bfloat16), 'band', split_ax...]
    dot_general x4 -> x0, matrix products: 11.7 us -> none  [the longest x1 5.95 us: per_device(): jnp.einsum('wpcf,tcf->wpt', surface_force, dft_table, preferred_element_t...]
    all_to_all x1 -> x0, blocking collectives: 11.2 us -> none  [per_device(): lax.all_to_all(radiation_modes, 'mode', split_axis=0, concat_axis=1, tile...]
    cos x1 -> x0, other arithmetic: 9.14 us -> none  [make_table(): table = jnp.stack([jnp.cos(angles), -jnp.sin(angles)], axis=1) * norming]
    all_gather x1 -> x0, blocking collectives: 6.23 us -> none  [per_device(): collected = lax.all_gather(forcing, 'mode', axis=1, tiled=True)]
  transfers between devices with their start and end apart: 4 -> 0, of which waited for: 4 -> 0; matrix products, arithmetic and copies ran while one was open for 0% -> 0% of each run, Pallas kernels for 0% -> 0%
where the time goes in v1:
time: 60.3 us; the launch traced here: 59.7 us
  Pallas kernels  55.7 us (92%)
  local copies, waits for them, and re-layouts  2.61 us (4%)
  other arithmetic  0.68 us (1%)
  between operations  0.68 us (1%)
    pallas_call x1, Pallas kernels, fused(): pl.pallas_call(functools.partial(fused_kernel, nb, nm), out_shape=jax.Sha...  55.7 us
    unnamed x3, local copies, waits for them, and re-layouts  2.53 us

profile of v1, /device:TPU:0, one launch (start us, length us, event | category | flops | bytes accessed | tf_op | source)
XLA Modules:
  0.0 59.7 jit_solution(11974684695894821966)
XLA Ops:
  0.7 0.0 copy-start
  0.7 0.7 %copy-done = s32[512]{0:T(512)S(1)} copy-done((s32[512]{0:T(512)S(1)}, s32[512]{0:T(512)}, u32[]{:S(2)}) %copy-start) | copy-done | bytes 2072
  1.3 0.1 reshape.14
  1.4 0.7 %pad_add_fusion.freq_ref = s32[9,1,128]{2,1,0:T(1,128)} fusion(s32[1,1,128]{2,1,0:T(1,128)S(1)} %compare_select_fusion, s32[8,1,64]{2,1,0:T(1,128)S(1)} %reshape.14), kind=kLoop, calls=%fused_computation | loop fusion | flops 2304 | bytes 7168 | tf_op jit(solution)/shard_map/concatenate | solution.py:274
  2.1 55.7 %shard_map.55 = bf16[256,1024]{1,0:T(8,128)(2,1)} custom-call(bf16[256,1024]{1,0:T(8,128)(2,1)} %bitcast.5, bf16[1024,256]{1,0:T(8,128)(2,1)} %modes_ref.1, f32[1024,256]{1,0:T(8,128)} %bitcast.4, s32[1]{0:T(128)S(6)} %copy.7.rank_ref, s32[9,1,128]{2,1,0:T(1,128)} %pad_add_fusion.freq_ref), custom_call_target="tpu_custom_call" | custom-call | tf_op jit(solution)/shard_map/pallas_call | solution.py:278
  57.8 1.9 %copy.8 = bf16[1,256,1024]{2,1,0:T(8,128)(2,1)} copy(bf16[1,256,1024]{2,1,0:T(8,128)(2,1)} %bitcast.3) | data formatting | bytes 1048576
  (1 shorter events, 0.0 us)
Async XLA Ops:
  0.7 0.7 %copy-start = (s32[512]{0:T(512)S(1)}, s32[512]{0:T(512)}, u32[]{:S(2)}) copy-start(s32[512]{0:T(512)} %param.9) | copy-start | bytes 6148

commit v2 on v1

--- a/solution.py
+++ b/solution.py
@@ -26,20 +26,11 @@
     return jnp.where(flip, -value, value)
 
 
-def ordered_offsets(n):
-    offsets = [0]
-    for step in range(1, n // 2 + 1):
-        offsets.append(step)
-        if n - step != step:
-            offsets.append(n - step)
-    return offsets[:n]
-
-
 def fused_kernel(
     nb, nm, vel_ref, modes_ref, res_ref, rank_ref, freq_ref, out_ref,
-    table, trig, modes_t, res_hi, res_lo, spec, part, rs, coef, force, basis, acc,
-    bar_unused, sx_s, sx_r, sm_s, sm_r, sf_s, sf_r, rs_s, rs_r, k_s, k_r, ob_s, ob_r,
-    f_s, f_r, fx_s, fx_r, fm_s, fm_r, ff_s, ff_r,
+    table, trig, modes_t, res_hi, res_lo, spec, part, pair, rs, coef, force, basis, acc,
+    sx_s, sx_r, sm_s, sm_r, sf_s, sf_r, rs_s, rs_r, ry_s, ry_r, k_s, k_r, ob_s, ob_r,
+    fz_s, fz_r, fy_s, fy_r, fx_s, fx_r, gy_s, gy_r, gx_s, gx_r, fm_s, fm_r, ff_s, ff_r,
 ):
     b = lax.axis_index("band")
     m = lax.axis_index("mode")
@@ -50,8 +41,9 @@
     cols = table.shape[2]
     mode_cols = modes_ref.shape[1]
 
-    def band_at(offset):
-        return (b + offset) % nb
+    def band_at(e):
+        bits = [1 << i for i in range(nb.bit_length() - 1)]
+        return sum(bit * ((b // bit + e // bit) % 2) for bit in bits)
 
     def to_mode(src, dst, send, recv, target):
         return pltpu.make_async_remote_copy(
@@ -73,8 +65,11 @@
     norming = 1.0 / math.sqrt(steps)
 
     def build(k):
-        freq = freq_ref[k]
-        shift = freq_ref[nb]
+        half = cols // 2
+        lane = lax.broadcasted_iota(jnp.int32, (HALF_ROWS, cols), 1)
+        row = jnp.broadcast_to(freq_ref[pl.ds(k // 2, 1), :], (HALF_ROWS, cols))
+        freq = jnp.where(lane // half == k % 2, row, pltpu.roll(row, half, 1))
+        shift = jnp.where(lane < half, 0, steps // 4)
         rows = lax.broadcasted_iota(jnp.int32, (HALF_ROWS, cols), 0)
         big = lax.broadcasted_iota(jnp.int32, (blocks, cols), 0) * HALF_ROWS
         low = rows * freq + shift
@@ -94,8 +89,7 @@
             vel_ref[...], table[k], preferred_element_type=jnp.float32
         ).astype(jnp.bfloat16)
 
-    order = [(i + 1) % nb for i in range(nb)]
-    spectra(band_at(order[0]))
+    spectra(band_at(nb - 1))
     pl.semaphore_wait(barrier, nm - 1 + nb - 1)
 
     def s_cross(k):
@@ -108,17 +102,17 @@
         return to_mode(spec.at[k, cross], spec.at[k, cross], sf_s.at[k], sf_r.at[k], mate)
 
     def spec_step(i, _):
-        k = (b + 1 + i) % nb
+        k = band_at(nb - 1 - i)
         s_cross(k).start()
         s_mate(k).start()
-
-        nxt = (b + 2 + i) % nb
-        spectra(nxt)
+        spectra(band_at(nb - 2 - i))
         return 0
 
     lax.fori_loop(0, nb - 1, spec_step, 0)
     s_cross(b).start()
     s_mate(b).start()
+
+    near = band_at(1)
 
     def basis_copy(off):
         target = (m + off) % nm
@@ -128,86 +122,139 @@
     for off in range(1, nm):
         basis_copy(off).start()
     modes_t[...] = modes_ref[...].T
-
-    def partial(k):
-        return jnp.dot(
-            modes_t[...], spec[k].reshape(nm * patches, cols), preferred_element_type=jnp.float32)
-
-    def rs_copy(k):
-        return to_band(part.at[k], rs.at[b], rs_s.at[k], rs_r.at[b], k)
-
-    def rs_arrival(k):
-        return to_band(part.at[k], rs.at[k], rs_s.at[k], rs_r.at[k], k)
-
-    def arrive(k):
-        s_cross(k).wait_recv()
-        s_fwd(k).start()
-
-    def finish(k):
-        s_mate(k).wait_recv()
-        s_fwd(k).wait_recv()
-
-    def part_step(i, _):
-        k = (b + 1 + i) % nb
-        arrive((b + 2 + i) % nb)
-        finish(k)
-        part[k] = partial(k).astype(jnp.bfloat16)
-        rs_copy(k).start()
-        return 0
-
-    arrive(band_at(1))
-    lax.fori_loop(0, nb - 1, part_step, 0)
     wide = res_ref[...].T
     narrow = wide.astype(jnp.bfloat16)
     res_hi[...] = narrow
     res_lo[...] = (wide - narrow.astype(jnp.float32)).astype(jnp.bfloat16)
+
+    def partial(k):
+        return jnp.dot(
+            modes_t[...], spec[k].reshape(nm * patches, cols), preferred_element_type=jnp.float32)
+
+    def rs_copy(k):
+        return to_band(part.at[k], rs.at[b], rs_s.at[k], rs_r.at[b], k)
+
+    def rs_arrival(k):
+        return to_band(part.at[k], rs.at[k], rs_s.at[k], rs_r.at[k], k)
+
+    def arrive(k):
+        s_cross(k).wait_recv()
+        s_fwd(k).start()
+
+    def finish(k):
+        s_mate(k).wait_recv()
+        s_fwd(k).wait_recv()
+
+    def pair_copy(k):
+        return to_band(part.at[k], pair.at[k], ry_s.at[k], ry_r.at[k], near)
+
+    def with_pair(k):
+        value = partial(k)
+        pair_copy(k).wait_recv()
+        return value + pair[k].astype(jnp.float32)
+
+    def part_step(i, _):
+        e = nb - 1 - 2 * i
+        other, mine = band_at(e), band_at(e - 1)
+        arrive(mine)
+        finish(other)
+        part[other] = partial(other).astype(jnp.bfloat16)
+        pair_copy(other).start()
+        arrive(band_at(e - 2))
+        finish(mine)
+        part[mine] = with_pair(mine).astype(jnp.bfloat16)
+        rs_copy(mine).start()
+        return 0
+
+    arrive(band_at(nb - 1))
+    lax.fori_loop(0, nb // 2 - 1, part_step, 0)
+    arrive(b)
+    finish(near)
+    part[near] = partial(near).astype(jnp.bfloat16)
+    pair_copy(near).start()
     finish(b)
-    total = partial(b)
-    for off in range(1, nb):
-        k = band_at(nb - off)
+    total = with_pair(b)
+    for e in range(nb - 2, 0, -2):
+        k = band_at(e)
         rs_arrival(k).wait_recv()
         total = total + rs[k].astype(jnp.float32)
-    kept = lax.broadcasted_iota(jnp.int32, (mode_cols, cols), 0) + m * mode_cols < rank_ref[0]
+    kept = lax.broadcasted_iota(jnp.int32, (mode_cols, cols), 0) + m * mode_cols < rank_ref[...]
     total = jnp.where(kept, total, 0.0)
     coef[m] = total.astype(jnp.bfloat16)
 
-    def k_copy(off):
-        return to_mode(coef.at[m], coef.at[m], k_s.at[off], k_r.at[off], (m + off) % nm)
-
-    def k_arrival(off):
-        source = (m + nm - off) % nm
-        return to_mode(coef.at[source], coef.at[source], k_s.at[off], k_r.at[off], source)
-
-    for off in range(1, nm):
-        k_copy(off).start()
-    for off in range(1, nm):
-        k_arrival(off).wait_recv()
+    k_copies = [
+        to_mode(coef.at[slot], coef.at[slot], k_s.at[i], k_r.at[i], target)
+        for i, (slot, target) in enumerate([(m, cross), (m, mate), (cross, mate)])
+    ]
+    k_copies[0].start()
+    k_copies[1].start()
+    k_copies[0].wait_recv()
+    k_copies[2].start()
+    k_copies[1].wait_recv()
+    k_copies[2].wait_recv()
     coefs = coef[...].reshape(nm * mode_cols, cols)
     forcing = jnp.dot(res_hi[...], coefs, preferred_element_type=jnp.float32) + jnp.dot(
         res_lo[...], coefs, preferred_element_type=jnp.float32)
     forcing = jnp.where(kept, 2.0 * forcing, 0.0)
     force[b, m] = forcing.astype(jnp.bfloat16)
 
-    def f_copy(k):
-        return to_band(force.at[b, m], force.at[b, m], f_s.at[k], f_r.at[b], k)
-
-    def f_arrival(k):
-        return to_band(force.at[k, m], force.at[k, m], f_s.at[k], f_r.at[k], k)
+    half = mode_cols // 2
+    upper, lower = pl.ds(0, half), pl.ds(half, half)
+
+    def f_far(k):
+        return to_band(force.at[b, m], force.at[b, m], fz_s.at[k], fz_r.at[b], k)
+
+    def f_far_arrival(k):
+        return to_band(force.at[k, m], force.at[k, m], fz_s.at[k], fz_r.at[k], k)
+
+    def f_near(k):
+        return to_band(force.at[k, m], force.at[k, m], fy_s.at[k], fy_r.at[k], near)
 
     def f_cross(k):
         return to_mode(force.at[k, m], force.at[k, m], fx_s.at[k], fx_r.at[k], cross)
 
+    def g_near(k):
+        piece = force.at[k, cross, lower]
+        return to_band(piece, piece, gy_s.at[k], gy_r.at[k], near)
+
+    def g_cross(k):
+        piece = force.at[k, m, upper]
+        return to_mode(piece, piece, gx_s.at[k], gx_r.at[k], cross)
+
     def f_mate(k):
         return to_mode(force.at[k, m], force.at[k, m], fm_s.at[k], fm_r.at[k], mate)
 
     def f_fwd(k):
         return to_mode(force.at[k, cross], force.at[k, cross], ff_s.at[k], ff_r.at[k], mate)
 
-    offsets = ordered_offsets(nb)
-    for off in offsets[1:]:
-        f_copy(band_at(off)).start()
-    f_cross(b).start()
-    f_mate(b).start()
+    far = list(range(0, nb, 2))
+
+    def first(j):
+        k = band_at(far[j])
+        if j > 0:
+            f_far_arrival(k).wait_recv()
+        f_near(k).start()
+        f_cross(k).start()
+        f_mate(k).start()
+
+    def second(j):
+        k, k1 = band_at(far[j]), band_at(far[j] + 1)
+        f_near(k1).wait_recv()
+        g_cross(k1).start()
+        f_mate(k1).start()
+        f_cross(k).wait_recv()
+        g_near(k).start()
+        f_fwd(k).start()
+
+    def third(j):
+        k1 = band_at(far[j] + 1)
+        g_cross(k1).wait_recv()
+        g_near(k1).wait_recv()
+        f_fwd(k1).start()
+
+    for e in far[1:]:
+        f_far(band_at(e)).start()
+    first(0)
 
     for off in range(1, nm):
         source = (m + nm - off) % nm
@@ -226,39 +273,48 @@
         return lax.dot_general(
             surface(k), table[k], (((1,), (1,)), ((), ())), preferred_element_type=jnp.float32)
 
-    for i in range(nb + 2):
-        if 1 <= i < nb:
-            k = band_at(offsets[i])
-            f_arrival(k).wait_recv()
-            f_cross(k).start()
-            f_mate(k).start()
-        if 1 <= i <= nb:
-            k = band_at(offsets[i - 1])
-            f_cross(k).wait_recv()
-            f_fwd(k).start()
-        if i >= 2:
-            k = band_at(offsets[i - 2])
-            term = history(k)
-            if i == 2:
-                acc[...] = term
-            elif i < nb + 1:
-                acc[...] += term
-            else:
-                out_ref[...] = (acc[...] + term).astype(out_ref.dtype)
+    def last(e):
+        term = history(band_at(e))
+        if e == 0:
+            acc[...] = term
+        elif e < nb - 1:
+            acc[...] += term
+        else:
+            out_ref[...] = (acc[...] + term).astype(out_ref.dtype)
+
+    n = len(far)
+    for j in range(1, n):
+        first(j)
+    for j in range(n):
+        second(j)
+    for j in range(n - 1):
+        last(far[j])
+        third(j)
+    third(n - 1)
+    last(far[n - 1])
+    for j in range(n):
+        last(far[j] + 1)
 
     def drain(k, _):
-        for copy in (s_cross, s_mate, s_fwd, f_cross, f_mate, f_fwd):
+        for copy in (s_cross, s_mate, s_fwd, f_mate, f_fwd):
             copy(k).wait_send()
         return 0
 
     lax.fori_loop(0, nb, drain, 0)
-    for off in range(1, nb):
-        k = band_at(off)
-        rs_copy(k).wait_send()
-        f_copy(k).wait_send()
+    for e in far:
+        k, k1 = band_at(e), band_at(e + 1)
+        pair_copy(k1).wait_send()
+        if e > 0:
+            f_far(k).wait_send()
+            rs_copy(k).wait_send()
+        f_near(k).wait_send()
+        f_cross(k).wait_send()
+        g_near(k).wait_send()
+        g_cross(k1).wait_send()
     for off in range(1, nm):
         basis_copy(off).wait_send()
-        k_copy(off).wait_send()
+    for copy in k_copies:
+        copy.wait_send()
 
 
 def fused(mesh, velocity, radiation_modes, resistance, mode_ranks, freq_table):
@@ -266,19 +322,14 @@
     patches, steps = velocity.shape[1:]
     mode_cols = radiation_modes.shape[1]
     modes = nm * mode_cols
-    slots = freq_table.shape[0] // nb
-    cols = 2 * slots
-    by_band = freq_table.reshape(nb, 1, slots)
-    freq_cols = jnp.concatenate([by_band, by_band], axis=2)
-    shift = jnp.where(jnp.arange(cols, dtype=jnp.int32) < slots, 0, steps // 4)
-    freq_cols = jnp.concatenate([freq_cols, shift.reshape(1, 1, cols).astype(jnp.int32)], axis=0)
+    cols = 2 * (freq_table.shape[0] // nb)
     bf16, f32 = jnp.bfloat16, jnp.float32
     dma = lambda n: pltpu.SemaphoreType.DMA((n,))
     vmem = pl.BlockSpec(memory_space=pltpu.VMEM)
     out = pl.pallas_call(
         functools.partial(fused_kernel, nb, nm),
         out_shape=jax.ShapeDtypeStruct((patches, steps), bf16),
-        in_specs=[vmem, vmem, vmem, pl.BlockSpec(memory_space=pltpu.SMEM), vmem],
+        in_specs=[vmem] * 5,
         out_specs=vmem,
         scratch_shapes=[
             pltpu.VMEM((nb, steps, cols), bf16),
@@ -289,17 +340,17 @@
             pltpu.VMEM((nb, nm, patches, cols), bf16),
             pltpu.VMEM((nb, mode_cols, cols), bf16),
             pltpu.VMEM((nb, mode_cols, cols), bf16),
+            pltpu.VMEM((nb, mode_cols, cols), bf16),
             pltpu.VMEM((nm, mode_cols, cols), bf16),
             pltpu.VMEM((nb, nm, mode_cols, cols), bf16),
             pltpu.VMEM((nm, patches, mode_cols), bf16),
             pltpu.VMEM((patches, steps), f32),
-            pltpu.SemaphoreType.REGULAR,
-        ]
-        + [dma(nb) for _ in range(8)]
+            ]
+        + [dma(nb) for _ in range(10)]
         + [dma(nm) for _ in range(4)]
-        + [dma(nb) for _ in range(8)],
+        + [dma(nb) for _ in range(14)],
         compiler_params=pltpu.CompilerParams(collective_id=0, has_side_effects=True),
-    )(velocity[0], radiation_modes, resistance[0], mode_ranks, freq_cols)
+    )(velocity[0], radiation_modes, resistance[0], mode_ranks.reshape(1, 1), freq_table.reshape(nb // 2, cols))
     return out[None]
 
 
@@ -378,7 +429,7 @@
         mode_cols = radiation_modes.shape[1]
         cols = 2 * (freq_table.shape[0] // nb)
         tiled = (
-            windows == 1 and nm == 4 and nb > 1 and cols % 128 == 0 and mode_cols % 128 == 0
+            windows == 1 and nm == 4 and nb > 2 and nb & (nb - 1) == 0 and cols == 128 and mode_cols % 128 == 0
             and patches % 128 == 0 and steps % 128 == 0 and steps & (steps - 1) == 0
         )
         args = (velocity, radiation_modes, resistance, mode_ranks, freq_table)

time: 60.3 us -> 54.5 us (0.904)
  Pallas kernels: 55.7 us -> 51.8 us
  local copies, waits for them, and re-layouts: 2.61 us -> 1.87 us
  other arithmetic: 0.68 us -> 0 us
    pallas_call x1, Pallas kernels: 55.7 us -> 51.8 us  [fused(): pl.pallas_call(functools.partial(fused_kernel, nb, nm), out_shape=jax.Sha...]
    concatenate x1 -> x0, other arithmetic: 0.67 us -> none  [fused(): jnp.concatenate([freq_cols, shift.reshape(1, 1, cols).astype(jnp.int32)],...]
    unnamed x3 -> x1, local copies, waits for them, and re-layouts: 2.53 us -> 1.87 us
where the time goes in v2:
time: 54.5 us; the launch traced here: 54.3 us
  Pallas kernels  51.8 us (95%)
  local copies, waits for them, and re-layouts  1.87 us (3%)
  between operations  0.66 us (1%)
    pallas_call x1, Pallas kernels, fused(): pl.pallas_call(functools.partial(fused_kernel, nb, nm), out_shape=jax.Sha...  51.8 us
    unnamed x1, local copies, waits for them, and re-layouts  1.87 us

profile of v2, /device:TPU:0, one launch (start us, length us, event | category | flops | bytes accessed | tf_op | source)
XLA Modules:
  0.0 54.3 jit_solution(9937275930055921721)
XLA Ops:
  0.7 51.8 %shard_map.55 = bf16[256,1024]{1,0:T(8,128)(2,1)} custom-call(bf16[256,1024]{1,0:T(8,128)(2,1)} %bitcast.8, bf16[1024,256]{1,0:T(8,128)(2,1)} %modes_ref.1, f32[1024,256]{1,0:T(8,128)} %bitcast.7, s32[1,1]{1,0:T(1,128)} %bitcast.5.rank_ref, s32[4,128]{1,0:T(4,128)} %bitcast.9), custom_call_target="tpu_custom_call" | custom-call | tf_op jit(solution)/shard_map/pallas_call | solution.py:329
  52.5 1.9 %copy.8 = bf16[1,256,1024]{2,1,0:T(8,128)(2,1)} copy(bf16[1,256,1024]{2,1,0:T(8,128)(2,1)} %bitcast.6) | data formatting | bytes 1048576

commit v3 on v2

--- a/solution.py
+++ b/solution.py
@@ -28,8 +28,8 @@
 
 def fused_kernel(
     nb, nm, vel_ref, modes_ref, res_ref, rank_ref, freq_ref, out_ref,
-    table, trig, modes_t, res_hi, res_lo, spec, part, pair, rs, coef, force, basis, acc,
-    sx_s, sx_r, sm_s, sm_r, sf_s, sf_r, rs_s, rs_r, ry_s, ry_r, k_s, k_r, ob_s, ob_r,
+    table, trig, modes_t, res_hi, res_lo, spec, part, rs, coef, force, basis, acc,
+    sx_s, sx_r, sm_s, sm_r, sf_s, sf_r, rs_s, rs_r, k_s, k_r, ob_s, ob_r,
     fz_s, fz_r, fy_s, fy_r, fx_s, fx_r, gy_s, gy_r, gx_s, gx_r, fm_s, fm_r, ff_s, ff_r,
 ):
     b = lax.axis_index("band")
@@ -90,6 +90,11 @@
         ).astype(jnp.bfloat16)
 
     spectra(band_at(nb - 1))
+    modes_t[...] = modes_ref[...].T
+    wide = res_ref[...].T
+    narrow = wide.astype(jnp.bfloat16)
+    res_hi[...] = narrow
+    res_lo[...] = (wide - narrow.astype(jnp.float32)).astype(jnp.bfloat16)
     pl.semaphore_wait(barrier, nm - 1 + nb - 1)
 
     def s_cross(k):
@@ -112,8 +117,6 @@
     s_cross(b).start()
     s_mate(b).start()
 
-    near = band_at(1)
-
     def basis_copy(off):
         target = (m + off) % nm
         rows = pl.ds(pl.multiple_of(target * patches, patches), patches)
@@ -121,12 +124,6 @@
 
     for off in range(1, nm):
         basis_copy(off).start()
-    modes_t[...] = modes_ref[...].T
-    wide = res_ref[...].T
-    narrow = wide.astype(jnp.bfloat16)
-    res_hi[...] = narrow
-    res_lo[...] = (wide - narrow.astype(jnp.float32)).astype(jnp.bfloat16)
-
     def partial(k):
         return jnp.dot(
             modes_t[...], spec[k].reshape(nm * patches, cols), preferred_element_type=jnp.float32)
@@ -145,53 +142,37 @@
         s_mate(k).wait_recv()
         s_fwd(k).wait_recv()
 
-    def pair_copy(k):
-        return to_band(part.at[k], pair.at[k], ry_s.at[k], ry_r.at[k], near)
-
-    def with_pair(k):
-        value = partial(k)
-        pair_copy(k).wait_recv()
-        return value + pair[k].astype(jnp.float32)
-
     def part_step(i, _):
-        e = nb - 1 - 2 * i
-        other, mine = band_at(e), band_at(e - 1)
-        arrive(mine)
-        finish(other)
-        part[other] = partial(other).astype(jnp.bfloat16)
-        pair_copy(other).start()
-        arrive(band_at(e - 2))
-        finish(mine)
-        part[mine] = with_pair(mine).astype(jnp.bfloat16)
-        rs_copy(mine).start()
+        k = band_at(nb - 1 - i)
+        arrive(band_at(nb - 2 - i))
+        finish(k)
+        part[k] = partial(k).astype(jnp.bfloat16)
+        rs_copy(k).start()
         return 0
 
     arrive(band_at(nb - 1))
-    lax.fori_loop(0, nb // 2 - 1, part_step, 0)
-    arrive(b)
-    finish(near)
-    part[near] = partial(near).astype(jnp.bfloat16)
-    pair_copy(near).start()
+    lax.fori_loop(0, nb - 1, part_step, 0)
     finish(b)
-    total = with_pair(b)
-    for e in range(nb - 2, 0, -2):
-        k = band_at(e)
+    total = partial(b)
+    for off in range(1, nb):
+        k = band_at(nb - off)
         rs_arrival(k).wait_recv()
         total = total + rs[k].astype(jnp.float32)
     kept = lax.broadcasted_iota(jnp.int32, (mode_cols, cols), 0) + m * mode_cols < rank_ref[...]
     total = jnp.where(kept, total, 0.0)
     coef[m] = total.astype(jnp.bfloat16)
 
-    k_copies = [
-        to_mode(coef.at[slot], coef.at[slot], k_s.at[i], k_r.at[i], target)
-        for i, (slot, target) in enumerate([(m, cross), (m, mate), (cross, mate)])
-    ]
-    k_copies[0].start()
-    k_copies[1].start()
-    k_copies[0].wait_recv()
-    k_copies[2].start()
-    k_copies[1].wait_recv()
-    k_copies[2].wait_recv()
+    def k_copy(off):
+        return to_mode(coef.at[m], coef.at[m], k_s.at[off], k_r.at[off], (m + off) % nm)
+
+    def k_arrival(off):
+        source = (m + nm - off) % nm
+        return to_mode(coef.at[source], coef.at[source], k_s.at[off], k_r.at[off], source)
+
+    for off in range(1, nm):
+        k_copy(off).start()
+    for off in range(1, nm):
+        k_arrival(off).wait_recv()
     coefs = coef[...].reshape(nm * mode_cols, cols)
     forcing = jnp.dot(res_hi[...], coefs, preferred_element_type=jnp.float32) + jnp.dot(
         res_lo[...], coefs, preferred_element_type=jnp.float32)
@@ -200,6 +181,7 @@
 
     half = mode_cols // 2
     upper, lower = pl.ds(0, half), pl.ds(half, half)
+    near = band_at(1)
 
     def f_far(k):
         return to_band(force.at[b, m], force.at[b, m], fz_s.at[k], fz_r.at[b], k)
@@ -301,20 +283,20 @@
         return 0
 
     lax.fori_loop(0, nb, drain, 0)
+    for off in range(1, nb):
+        k = band_at(off)
+        rs_copy(k).wait_send()
     for e in far:
         k, k1 = band_at(e), band_at(e + 1)
-        pair_copy(k1).wait_send()
         if e > 0:
             f_far(k).wait_send()
-            rs_copy(k).wait_send()
         f_near(k).wait_send()
         f_cross(k).wait_send()
         g_near(k).wait_send()
         g_cross(k1).wait_send()
     for off in range(1, nm):
         basis_copy(off).wait_send()
-    for copy in k_copies:
-        copy.wait_send()
+        k_copy(off).wait_send()
 
 
 def fused(mesh, velocity, radiation_modes, resistance, mode_ranks, freq_table):
@@ -340,13 +322,12 @@
             pltpu.VMEM((nb, nm, patches, cols), bf16),
             pltpu.VMEM((nb, mode_cols, cols), bf16),
             pltpu.VMEM((nb, mode_cols, cols), bf16),
-            pltpu.VMEM((nb, mode_cols, cols), bf16),
             pltpu.VMEM((nm, mode_cols, cols), bf16),
             pltpu.VMEM((nb, nm, mode_cols, cols), bf16),
             pltpu.VMEM((nm, patches, mode_cols), bf16),
             pltpu.VMEM((patches, steps), f32),
             ]
-        + [dma(nb) for _ in range(10)]
+        + [dma(nb) for _ in range(8)]
         + [dma(nm) for _ in range(4)]
         + [dma(nb) for _ in range(14)],
         compiler_params=pltpu.CompilerParams(collective_id=0, has_side_effects=True),
@@ -429,7 +410,7 @@
         mode_cols = radiation_modes.shape[1]
         cols = 2 * (freq_table.shape[0] // nb)
         tiled = (
-            windows == 1 and nm == 4 and nb > 2 and nb & (nb - 1) == 0 and cols == 128 and mode_cols % 128 == 0
+            windows == 1 and nm == 4 and nb == 8 and cols == 128 and mode_cols % 128 == 0
             and patches % 128 == 0 and steps % 128 == 0 and steps & (steps - 1) == 0
         )
         args = (velocity, radiation_modes, resistance, mode_ranks, freq_table)

time: 54.5 us -> 53 us (0.972)
  Pallas kernels: 51.8 us -> 50.3 us
    pallas_call x1, Pallas kernels: 51.8 us -> 50.3 us  [fused(): pl.pallas_call(functools.partial(fused_kernel, nb, nm), out_shape=jax.Sha...]
where the time goes in v3:
time: 53 us; the launch traced here: 52.8 us
  Pallas kernels  50.3 us (95%)
  local copies, waits for them, and re-layouts  1.87 us (4%)
  between operations  0.66 us (1%)
    pallas_call x1, Pallas kernels, fused(): pl.pallas_call(functools.partial(fused_kernel, nb, nm), out_shape=jax.Sha...  50.3 us
    unnamed x1, local copies, waits for them, and re-layouts  1.87 us

profile of v3, /device:TPU:0, one launch (start us, length us, event | category | flops | bytes accessed | tf_op | source)
XLA Modules:
  0.0 52.8 jit_solution(4209343914937591640)
XLA Ops:
  0.7 50.3 %shard_map.55 = bf16[256,1024]{1,0:T(8,128)(2,1)} custom-call(bf16[256,1024]{1,0:T(8,128)(2,1)} %bitcast.8, bf16[1024,256]{1,0:T(8,128)(2,1)} %modes_ref.1, f32[1024,256]{1,0:T(8,128)} %bitcast.7, s32[1,1]{1,0:T(1,128)} %bitcast.5.rank_ref, s32[4,128]{1,0:T(4,128)} %bitcast.9), custom_call_target="tpu_custom_call" | custom-call | tf_op jit(solution)/shard_map/pallas_call | solution.py:311
  51.0 1.9 %copy.8 = bf16[1,256,1024]{2,1,0:T(8,128)(2,1)} copy(bf16[1,256,1024]{2,1,0:T(8,128)(2,1)} %bitcast.6) | data formatting | bytes 1048576
